TPU v7x, 256 devices: a whole 4x4x8 slice. The times are simulated.
256 devices in a mesh: ctx: 16 (over z, core), exp: 16 (over x, y).
Axes of the slice: x: 4, y: 4, z: 8, core: 2. Of those that a mesh axis runs over, the one named last changes fastest.
Arguments:
- queries: bfloat16 [2, 16384, 2560], P(None, ('ctx', 'exp'))
- key_states: bfloat16 [2, 16384, 512], P(None, ('ctx', 'exp'))
- value_state_rows: bfloat16 [2, 16384, 512], P(None, ('ctx', 'exp')), may hold values from -6 to 6
- block_lists: int32 [32], replicated, may hold values from 0 to 31, as said below
- hidden: bfloat16 [8192, 5120], P(('ctx', 'exp')), may hold values from -8 to 8
- router: bfloat16 [5120, 16], replicated, may hold values from -0.078125 to 0.078125
- expert_ids: int32 [8192, 1], P(('ctx', 'exp')), may hold values from 0 to 15; in each aligned block of 32 rows (0 to 31, 32 to 63, ...) at most 4 rows name the same one
- w_gate: bfloat16 [16, 5120, 4096], P('exp', None, 'ctx'), may hold values from -0.078125 to 0.078125
- w_up: bfloat16 [16, 5120, 4096], P('exp', None, 'ctx'), may hold values from -0.078125 to 0.078125
- w_down: bfloat16 [16, 4096, 5120], P('exp', 'ctx'), may hold values from -0.1875 to 0.1875
Outputs:
- attention: bfloat16 [2, 16384, 2560], P(None, ('ctx', 'exp'))
- moe_out: bfloat16 [8192, 5120], P(('ctx', 'exp'))
Inputs may be any that keep to these rules, and one draw needn't show every extreme that they name: block_lists[b] is a block before b, or b itself when block b attends only to its own keys (always for b = 0 and for b = 31). Block p is held by index min(p, 31 - p) of ctx; for each d < 16 with block_lists[d] != d and block_lists[31 - d] != 31 - d, the two listed blocks are held by different indices. `expert_ids`: among the rows of one device no expert is named more than 4 times.
All inputs are finite; a program needn't handle non-finite values.
Results may differ from a plain program's by a relative error of at most 0.023.
Values may be sent and summed in bfloat16 or wider, within the bound.
No kernel may reach another device: no remote copies, remote signals or barrier semaphores. Data moves between devices by JAX's collectives and lax.ppermute only.
A program may use at most 128 MiB of HBM per device.

v0:
```python
import jax
import jax.numpy as jnp
from jax import lax
from jax.sharding import PartitionSpec as P

QUERY_HEADS = 20
KEY_HEADS = 4
HEAD_DIM = 128
NEGATIVE_LARGE = -1e30


def attend_all(queries, key_states, value_state_rows, block_lists):
    ctx_count = lax.axis_size("ctx")
    blocks_total = 2 * ctx_count
    ctx_index = lax.axis_index("ctx")
    exp_index = lax.axis_index("exp")
    row_total_count = queries.shape[1]
    query_group_width = QUERY_HEADS // KEY_HEADS
    key_value_width = KEY_HEADS * HEAD_DIM
    paired = jnp.concatenate([key_states, value_state_rows], axis=2)
    own_blocks = jnp.stack([ctx_index, blocks_total - 1 - ctx_index])
    listed = block_lists[own_blocks]
    usable = listed != own_blocks
    holder = jnp.minimum(listed, blocks_total - 1 - listed)
    everyone = lax.all_gather(paired[None], "ctx", axis=0, tiled=True)
    second_half = (listed >= ctx_count).astype(jnp.int32)
    remote = everyone[holder, second_half]
    stacked = jnp.concatenate([paired, remote], axis=0)
    query_head_rows = queries.reshape(2, row_total_count, KEY_HEADS, query_group_width, HEAD_DIM)
    query_pos = exp_index * row_total_count + jnp.arange(row_total_count)
    scaling = HEAD_DIM ** (-0.5)
    piece_rows = lax.all_gather(stacked, "exp", axis=1, tiled=True)
    running_maximum = jnp.full(
        (2, KEY_HEADS, query_group_width, row_total_count), NEGATIVE_LARGE, jnp.float32
    )
    key_total_count = piece_rows.shape[1]
    concatenated_rows = jnp.concatenate([piece_rows[0:2], piece_rows[2:4]], axis=1)
    key_portion = concatenated_rows[..., :key_value_width].reshape(
        2, 2 * key_total_count, KEY_HEADS, HEAD_DIM
    )
    value_portion = concatenated_rows[..., key_value_width:].reshape(
        2, 2 * key_total_count, KEY_HEADS, HEAD_DIM
    )
    scores = (
        jnp.einsum(
            "prhgd,pkhd->phgrk", query_head_rows, key_portion, preferred_element_type=jnp.float32
        )
        * scaling
    )
    key_pos = jnp.arange(key_total_count)
    causal = jnp.broadcast_to(
        (key_pos[None, :] <= query_pos[:, None])[None], (2, row_total_count, key_total_count)
    )
    listed_ok = jnp.broadcast_to(usable[:, None, None], (2, row_total_count, key_total_count))
    allowed = jnp.concatenate([causal, listed_ok], axis=2)[:, None, None]
    masked = jnp.where(allowed, scores, NEGATIVE_LARGE)
    new_max = jnp.maximum(running_maximum, jnp.max(masked, axis=-1))
    weights = jnp.where(allowed, jnp.exp(masked - new_max[..., None]), 0.0)
    new_sum = jnp.sum(weights, axis=-1)
    update = jnp.einsum(
        "phgrk,pkhd->phgrd",
        weights.astype(jnp.bfloat16),
        value_portion,
        preferred_element_type=jnp.float32,
    )
    mixed_rows = update / new_sum[..., None]
    return (
        jnp.transpose(mixed_rows, (0, 3, 1, 2, 4))
        .reshape(2, row_total_count, QUERY_HEADS * HEAD_DIM)
        .astype(jnp.bfloat16)
    )


def route_experts(hidden, router, expert_ids, w_gate, w_up, w_down):
    expert_table = router.shape[1]
    local_tokens = hidden.shape[0]
    model_width = hidden.shape[1]
    capacity = max(2, 2 * local_tokens // expert_table)
    exp_count = lax.axis_size("exp")
    logits = jnp.dot(hidden, router, preferred_element_type=jnp.float32)
    selected_expert = expert_ids[:, 0]
    onehot = (selected_expert[:, None] == jnp.arange(expert_table)[None, :]).astype(jnp.float32)
    gate_score = jax.nn.sigmoid(jnp.sum(logits * onehot, axis=1))
    scaled_scores = (hidden.astype(jnp.float32) * gate_score[:, None]).astype(jnp.bfloat16)
    slot_rank = (jnp.sum(jnp.cumsum(onehot, axis=0) * onehot, axis=1) - 1.0).astype(jnp.int32)
    dispatch = (
        (selected_expert[None, None, :] == jnp.arange(expert_table)[:, None, None])
        & (slot_rank[None, None, :] == jnp.arange(capacity)[None, :, None])
    ).astype(jnp.bfloat16)
    gate_local = w_gate[0]
    up_local = w_up[0]
    down_local = w_down[0]
    outgoing = jnp.einsum(
        "ect,td->ecd", dispatch, scaled_scores, preferred_element_type=jnp.float32
    ).astype(jnp.bfloat16)
    incoming = lax.all_to_all(outgoing, "exp", split_axis=0, concat_axis=0, tiled=True)
    piece_rows = lax.all_gather(incoming.reshape(-1, model_width), "ctx", axis=0, tiled=True)
    gate_part = jnp.dot(piece_rows, gate_local, preferred_element_type=jnp.float32)
    up_part = jnp.dot(piece_rows, up_local, preferred_element_type=jnp.float32)
    hidden_activation = (jax.nn.silu(gate_part) * up_part).astype(jnp.bfloat16)
    summed_output = lax.psum_scatter(
        jnp.dot(hidden_activation, down_local, preferred_element_type=jnp.float32).astype(
            jnp.bfloat16
        ),
        "ctx",
        scatter_dimension=0,
        tiled=True,
    )
    returned = lax.all_to_all(
        summed_output.reshape(exp_count, capacity, model_width),
        "exp",
        split_axis=0,
        concat_axis=0,
        tiled=True,
    )
    return jnp.einsum("ect,ecd->td", dispatch, returned, preferred_element_type=jnp.float32).astype(
        jnp.bfloat16
    )


def shards(
    queries,
    key_states,
    value_state_rows,
    block_lists,
    hidden,
    router,
    expert_ids,
    w_gate,
    w_up,
    w_down,
):
    attention = attend_all(queries, key_states, value_state_rows, block_lists)
    moe_out = route_experts(hidden, router, expert_ids, w_gate, w_up, w_down)
    return (attention, moe_out)


def solution(mesh):
    placed = (
        P(None, ("ctx", "exp"), None),
        P(None, ("ctx", "exp"), None),
        P(None, ("ctx", "exp"), None),
        P(),
        P(("ctx", "exp"), None),
        P(),
        P(("ctx", "exp"), None),
        P("exp", None, "ctx"),
        P("exp", None, "ctx"),
        P("exp", "ctx", None),
    )
    return jax.shard_map(
        shards,
        mesh=mesh,
        in_specs=placed,
        out_specs=(P(None, ("ctx", "exp"), None), P(("ctx", "exp"), None)),
        check_vma=False,
    )
```

profile of v0, /device:TPU:2, one launch (start us, length us, event | category | flops | bytes accessed | tf_op | source)
XLA Modules:
  0.0 308.0 jit_solution(14980662462300857561)
XLA Ops:
  7.2 0.0 all-gather.9.cloned.1.call-start
  7.2 1.1 constant_dynamic-update-slice_fusion.1
  8.3 0.9 constant_dynamic-update-slice_fusion
  9.2 0.7 copy-done.2
  9.9 0.0 all-gather.9.cloned.1.call-update
  9.9 0.0 all-gather.7.cloned.1.call-start
  10.0 0.7 fusion.45
  10.7 0.1 copy.28
  10.7 0.1 reduce_window_sum.11
  10.8 0.1 copy.29
  10.9 0.7 select_reduce_fusion
  11.5 1.3 fusion.24
  12.9 0.7 iota_compare_fusion.2
  13.5 1.4 convolution_convert_fusion.1
  14.9 0.5 copy.30
  15.4 18.6 %all_to_all.10 = bf16[16,4,5120]{2,1,0:T(4,128)(2,1)S(1)} all-to-all(bf16[16,4,5120]{2,1,0:T(4,128)(2,1)S(1)} %copy.30), channel_id=1, replica_groups=mesh['ctx'=16,'exp'=16] {'exp'}, dimensions={0} | all-to-all | bytes 1310720 | tf_op jit(solution)/shard_map/all_to_all | solution.py:96
  34.0 1.0 reshape.252
  35.0 0.0 all-gather.7.cloned.1.call-update
  35.0 0.0 all-gather.5.cloned.1.call-start
  35.1 0.1 fusion.46
  35.2 1.3 gather_fusion
  36.5 19.3 %all-gather.9.cloned.1.call-done = bf16[32,64,1024]{2,1,0:T(8,128)(2,1)} async-done(((bf16[2,64,1024]{2,1,0:T(8,128)(2,1)}), bf16[32,64,1024]{2,1,0:T(8,128)(2,1)}) %all-gather.9.cloned.1.call-update) | async-done | bytes 4194320 | tf_op jit(solution)/shard_map/all_gather | solution.py:25
  55.8 2.8 gather_fusion.1
  58.5 1.8 pad_maximum_fusion.1
  60.3 0.0 all-gather.5.cloned.1.call-update
  60.3 0.0 reduce-scatter.2.cloned.1.call-start
  60.4 61.9 %all-gather.7.cloned.1.call-done = bf16[1024,5120]{1,0:T(8,128)(2,1)} async-done(((bf16[64,5120]{1,0:T(8,128)(2,1)}), bf16[1024,5120]{1,0:T(8,128)(2,1)}) %all-gather.7.cloned.1.call-update) | async-done | bytes 10485776 | tf_op jit(solution)/shard_map/all_gather | solution.py:97
  122.3 8.6 %fusion.11 = f32[1024,256]{1,0:T(8,128)} fusion(bf16[1024,5120]{1,0:T(8,128)(2,1)} %all-gather.7.cloned.1.call-done, bf16[1,5120,256]{2,1,0:T(8,128)(2,1)} %param.17), kind=kOutput, calls=%fused_computation.20 | convolution fusion | flops 2684354560 | bytes 14155776 | tf_op jit(solution)/shard_map/dot_general | solution.py:98
  130.9 21.1 %convolution_convert_fusion = bf16[1024,5120]{1,0:T(8,128)(2,1)} fusion(bf16[1,256,5120]{2,1,0:T(8,128)(2,1)S(1)} %copy-done, bf16[1024,5120]{1,0:T(8,128)(2,1)} %all-gather.7.cloned.1.call-done, bf16[1,5120,256]{2,1,0:T(8,128)(2,1)} %param.18, f32[1024,256]{1,0:T(8,128)} %fusion.11), kind=kOutput, calls=%fused_computation.9 | convolution fusion | flops 5375524864 | bytes 27262976 | tf_op jit(solution)/shard_map/dot_general | solution.py:102
  152.0 1.1 copy-done.3
  153.1 0.8 reshape.250
  153.9 0.1 add_compare_fusion
  153.9 0.1 iota_compare_fusion
  154.1 0.1 broadcast_in_dim.27
  154.2 44.9 %all-gather.5.cloned.1.call-done = bf16[4,1024,1024]{2,1,0:T(8,128)(2,1)} async-done(((bf16[4,64,1024]{2,1,0:T(8,128)(2,1)}), bf16[4,1024,1024]{2,1,0:T(8,128)(2,1)}) %all-gather.5.cloned.1.call-update) | async-done | bytes 8388624 | tf_op jit(solution)/shard_map/all_gather | solution.py:32
  199.1 3.9 %fusion.57 = (bf16[2,1024,1024]{2,1,0:T(8,128)(2,1)S(1)}, bf16[2,1024,1024]{2,1,0:T(8,128)(2,1)S(1)}) fusion(bf16[4,1024,1024]{2,1,0:T(8,128)(2,1)} %all-gather.5.cloned.1.call-done), kind=kLoop, calls=%fused_computation.78 | loop fusion | bytes 16777216 | tf_op jit(solution)/shard_map/slice | solution.py:37
  203.1 3.7 %fusion.7 = (bf16[2,2048,512]{2,1,0:T(8,128)(2,1)}, bf16[2,2048,512]{2,1,0:T(8,128)(2,1)}) fusion(bf16[2,1024,1024]{2,1,0:T(8,128)(2,1)S(1)} %get-tuple-element.4, bf16[2,1024,1024]{2,1,0:T(8,128)(2,1)S(1)} %get-tuple-element.5), kind=kLoop, calls=%fused_computation.15 | loop fusion | flops 16777216 | bytes 16777216 | tf_op jit(solution)/shard_map/concatenate | solution.py:37
  206.8 6.3 %copy.25 = bf16[2,2048,512]{1,2,0:T(8,128)(2,1)} copy(bf16[2,2048,512]{2,1,0:T(8,128)(2,1)} %get-tuple-element.3) | data formatting | bytes 8388608 | tf_op jit(solution)/shard_map/slice | solution.py:41
  213.1 6.3 %copy.22 = bf16[2,2048,512]{1,2,0:T(8,128)(2,1)} copy(bf16[2,2048,512]{2,1,0:T(8,128)(2,1)} %get-tuple-element.2) | data formatting | bytes 8388608 | tf_op jit(solution)/shard_map/slice | solution.py:38
  219.4 13.4 %fusion = (f32[2,4,5,64]{3,2,1,0:T(8,128)S(1)}, f32[2,4,2048,64,5]{2,3,4,1,0:T(8,128)}) fusion(pred[2,64,2048]{2,1,0:T(8,128)(4,1)S(1)} %pad_add_fusion, bf16[2,2048,4,128,1]{1,3,4,2,0:T(8,128)(2,1)} %bitcast.70, bf16[2,64,4,5,128]{4,3,2,1,0:T(8,128)(2,1)S(1)} %reshape.250), kind=kOutput, calls=%fused_computation.4 | convolution fusion | flops 1357903360 | bytes 26093568 | tf_op jit(solution)/shard_map/prhgd,pkhd->phgrk/dot_general | solution.py:45
  232.9 11.6 %fusion.1 = f32[2,4,5,64]{3,2,1,0:T(8,128)} fusion(f32[2,4,2048,64,5]{2,3,4,1,0:T(8,128)} %get-tuple-element.7, f32[2,4,5,64]{3,2,1,0:T(8,128)S(1)} %broadcast_maximum_fusion, pred[2,64,2048]{2,1,0:T(8,128)(4,1)S(1)} %pad_add_fusion), kind=kLoop, calls=%fused_computation.5 | loop fusion | flops 26211840 | bytes 21254144 | tf_op jit(solution)/shard_map/reduce_sum | solution.py:59
  244.5 31.3 %reduce-scatter.2.cloned.1.call-done = bf16[64,5120]{1,0:T(8,128)(2,1)} async-done(((bf16[1024,5120]{1,0:T(8,128)(2,1)}), bf16[64,5120]{1,0:T(8,128)(2,1)}) %reduce-scatter.2.cloned.1.call-update) | async-done | bytes 655376 | tf_op jit(solution)/shard_map/reduce_scatter | solution.py:101
  275.8 2.4 reshape.253
  278.2 7.4 %all-to-all-start.1 = ((bf16[16,4,5120]{2,1,0:T(4,128)(2,1)}), bf16[16,4,5120]{2,1,0:T(4,128)(2,1)S(1)}, u32[]{:S(2)}, u32[]{:S(2)}) async-start(bf16[16,4,5120]{2,1,0:T(4,128)(2,1)} %reshape.253), calls=%async_computation.2 | async-start | bytes 1310720 | tf_op jit(solution)/shard_map/all_to_all | solution.py:109
  285.5 10.9 %divide_convert_fusion = bf16[2,64,4,5,128]{4,1,3,2,0:T(8,128)(2,1)S(1)} fusion(bf16[2,2048,4,128,1]{1,3,4,2,0:T(8,128)(2,1)} %bitcast.71, f32[2,4,2048,64,5]{2,3,4,1,0:T(8,128)} %get-tuple-element.7, f32[2,4,5,64]{3,2,1,0:T(8,128)} %copy-done.4, pred[2,64,2048]{2,1,0:T(8,128)(4,1)S(1)} %pad_add_fusion, f32[2,64,4,5]{1,3,2,0:T(8,128)} %bitcast.72), kind=kOutput, calls=%fused_computation.23 | convolution fusion | flops 1369047040 | bytes 26103808 | tf_op jit(solution)/shard_map/phgrk,pkhd->phgrd/dot_general | solution.py:60
  296.4 1.4 copy.27
  297.9 2.6 convert_element_type.51
  300.4 1.0 fusion.6
  (19 shorter events, 0.1 us)
Async XLA Ops:
  7.2 123.7 %copy-start = (bf16[1,256,5120]{2,1,0:T(8,128)(2,1)S(1)}, bf16[1,256,5120]{2,1,0:T(8,128)(2,1)}, u32[]{:S(2)}) copy-start(bf16[1,256,5120]{2,1,0:T(8,128)(2,1)} %param.19) | copy-start | bytes 7864324
  7.2 48.6 %all-gather.9.cloned.1.call-start = ((), (), s32[]{:S(2)}) async-start(), calls=%async_computation.6 | async-start | bytes 4456448 | tf_op jit(solution)/shard_map/all_gather | solution.py:25
  9.2 0.7 copy-start.2
  9.9 112.4 %all-gather.7.cloned.1.call-start = ((), (), s32[]{:S(2)}) async-start(), calls=%async_computation.4 | async-start | bytes 11141120 | tf_op jit(solution)/shard_map/all_gather | solution.py:97
  35.0 164.1 %all-gather.5.cloned.1.call-start = ((), (), s32[]{:S(2)}) async-start(), calls=%async_computation.3 | async-start | bytes 8912896 | tf_op jit(solution)/shard_map/all_gather | solution.py:32
  60.3 215.5 %reduce-scatter.2.cloned.1.call-start = ((), (), s32[]{:S(2)}) async-start(), calls=%async_computation.5 | async-start | bytes 11141120 | tf_op jit(solution)/shard_map/reduce_scatter | solution.py:101
  152.0 1.1 copy-start.3
  232.9 11.6 %copy-start.4 = (f32[2,4,5,64]{3,2,1,0:T(8,128)}, f32[2,4,5,64]{3,2,1,0:T(8,128)S(1)}, u32[]{:S(2)}) copy-start(f32[2,4,5,64]{3,2,1,0:T(8,128)S(1)} %broadcast_maximum_fusion) | copy-start | bytes 30724
  278.2 22.3 %all-to-all-start.1 = ((bf16[16,4,5120]{2,1,0:T(4,128)(2,1)}), bf16[16,4,5120]{2,1,0:T(4,128)(2,1)S(1)}, u32[]{:S(2)}, u32[]{:S(2)}) async-start(bf16[16,4,5120]{2,1,0:T(4,128)(2,1)} %reshape.253), calls=%async_computation.2 | async-start | bytes 1310720 | tf_op jit(solution)/shard_map/all_to_all | solution.py:109
  285.5 15.9 %copy-start.1 = (bf16[1,256,5120]{2,1,0:T(8,128)(2,1)S(1)}, bf16[1,256,5120]{2,1,0:T(8,128)(2,1)}, u32[]{:S(2)}) copy-start(bf16[1,256,5120]{2,1,0:T(8,128)(2,1)} %param.19) | copy-start | bytes 7864324
Sparse Core Ops, SparseCore 0:
  10.4 45.3 all-gather.8
  58.2 64.0 all-gather.6
  124.8 74.2 all-gather.4
  201.5 74.1 reduce-scatter.1
where the time goes:
time: 309 us; the launch traced here: 308 us
  waiting for transfers between devices  157 us (51%)
  matrix products  57.7 us (19%)
  local copies, waits for them, and re-layouts  33.3 us (11%)
  other arithmetic  19.5 us (6%)
  blocking collectives  18.6 us (6%)
  between operations  13.9 us (4%)
  starting transfers between devices  7.54 us (2%)
    all_gather x1, waiting for transfers between devices, route_experts(): lax.all_gather(incoming.reshape(-1, model_width), 'ctx', axis=0, tiled=True)  61.9 us
    all_gather x1, waiting for transfers between devices, attend_all(): piece_rows = lax.all_gather(stacked, 'exp', axis=1, tiled=True)  44.9 us
    reduce_scatter x1, waiting for transfers between devices, route_experts(): lax.psum_scatter(jnp.dot(hidden_activation, down_local, preferred_element...  31.3 us
    dot_general x1, matrix products, route_experts(): jnp.dot(hidden_activation, down_local, preferred_element_type=jnp.float32)  21.1 us
    all_gather x1, waiting for transfers between devices, attend_all(): everyone = lax.all_gather(paired[None], 'ctx', axis=0, tiled=True)  19.3 us
    all_to_all x1, blocking collectives, route_experts(): lax.all_to_all(outgoing, 'exp', split_axis=0, concat_axis=0, tiled=True)  18.6 us
    dot_general x1, matrix products, attend_all(): jnp.einsum('prhgd,pkhd->phgrk', query_head_rows, key_portion, preferred_e...  13.4 us
    reduce_sum x1, other arithmetic, attend_all(): new_sum = jnp.sum(weights, axis=-1)  11.6 us
  transfers between devices with their start and end apart: 5, of which 4 were waited for; matrix products, arithmetic and copies ran while one was open for 34% of the time, Pallas kernels for 0%

commit v1 on v0

--- a/solution.py
+++ b/solution.py
@@ -94,7 +94,12 @@
         "ect,td->ecd", dispatch, scaled_scores, preferred_element_type=jnp.float32
     ).astype(jnp.bfloat16)
     incoming = lax.all_to_all(outgoing, "exp", split_axis=0, concat_axis=0, tiled=True)
-    piece_rows = lax.all_gather(incoming.reshape(-1, model_width), "ctx", axis=0, tiled=True)
+    piece_rows = jnp.concatenate(
+        lax.all_to_all(
+            jnp.stack([incoming.reshape(-1, model_width)] * lax.axis_size("ctx")), "ctx", 0, 0
+        ),
+        axis=0,
+    )
     gate_part = jnp.dot(piece_rows, gate_local, preferred_element_type=jnp.float32)
     up_part = jnp.dot(piece_rows, up_local, preferred_element_type=jnp.float32)
     hidden_activation = (jax.nn.silu(gate_part) * up_part).astype(jnp.bfloat16)

time: 309 us -> 414 us (1.34)
  waiting for transfers between devices: 157 us -> 249 us
  starting transfers between devices: 7.54 us -> 16.2 us
  local copies, waits for them, and re-layouts: 33.3 us -> 39.1 us
    all_to_all x0 -> x1, waiting for transfers between devices: none -> 196 us  [route_experts(): lax.all_to_all(jnp.stack([incoming.reshape(-1, model_width)] * lax.axis_s...]
    all_gather x1 -> x0, waiting for transfers between devices: 61.9 us -> none  [route_experts(): lax.all_gather(incoming.reshape(-1, model_width), 'ctx', axis=0, tiled=True)]
    all_gather x1, waiting for transfers between devices: 44.9 us -> 0.02 us  [attend_all(): piece_rows = lax.all_gather(stacked, 'exp', axis=1, tiled=True)]
    all_gather x1, waiting for transfers between devices: 19.3 us -> 29 us  [attend_all(): everyone = lax.all_gather(paired[None], 'ctx', axis=0, tiled=True)]
    all_to_all x0 -> x1, starting transfers between devices: none -> 8.75 us  [route_experts(): lax.all_to_all(jnp.stack([incoming.reshape(-1, model_width)] * lax.axis_s...]
    another operation x0 -> x2, local copies, waits for them, and re-layouts: none -> 7.44 us  [route_experts(): jnp.stack([incoming.reshape(-1, model_width)] * lax.axis_size('ctx'))]
    reduce_scatter x1, waiting for transfers between devices: 31.3 us -> 24.5 us  [route_experts(): lax.psum_scatter(jnp.dot(hidden_activation, down_local, preferred_element...]
  transfers between devices with their start and end apart: 5 -> 5, of which waited for: 4 -> 3; matrix products, arithmetic and copies ran while one was open for 34% -> 26% of each run, Pallas kernels for 0% -> 0%
where the time goes in v1:
time: 414 us; the launch traced here: 413 us
  waiting for transfers between devices  249 us (60%)
  matrix products  57.5 us (14%)
  local copies, waits for them, and re-layouts  39.1 us (9%)
  other arithmetic  18.8 us (5%)
  blocking collectives  18.6 us (4%)
  starting transfers between devices  16.2 us (4%)
  between operations  13.9 us (3%)
    all_to_all x1, waiting for transfers between devices, route_experts(): lax.all_to_all(jnp.stack([incoming.reshape(-1, model_width)] * lax.axis_s...  196 us
    all_gather x1, waiting for transfers between devices, attend_all(): everyone = lax.all_gather(paired[None], 'ctx', axis=0, tiled=True)  29 us
    reduce_scatter x1, waiting for transfers between devices, route_experts(): lax.psum_scatter(jnp.dot(hidden_activation, down_local, preferred_element...  24.5 us
    dot_general x1, matrix products, route_experts(): jnp.dot(hidden_activation, down_local, preferred_element_type=jnp.float32)  21 us
    all_to_all x1, blocking collectives, route_experts(): lax.all_to_all(outgoing, 'exp', split_axis=0, concat_axis=0, tiled=True)  18.6 us
    dot_general x1, matrix products, attend_all(): jnp.einsum('prhgd,pkhd->phgrk', query_head_rows, key_portion, preferred_e...  13.4 us
    reduce_sum x1, other arithmetic, attend_all(): new_sum = jnp.sum(weights, axis=-1)  11.6 us
    dot_general x1, matrix products, attend_all(): jnp.einsum('phgrk,pkhd->phgrd', weights.astype(jnp.bfloat16), value_porti...  10.9 us
  transfers between devices with their start and end apart: 5, of which 3 were waited for; matrix products, arithmetic and copies ran while one was open for 26% of the time, Pallas kernels for 0%

profile of v1, /device:TPU:2, one launch (start us, length us, event | category | flops | bytes accessed | tf_op | source)
XLA Modules:
  0.0 413.3 jit_solution(9780575110425472419)
XLA Ops:
  7.2 0.0 all-gather.6.cloned.1.call-start
  7.2 1.1 constant_dynamic-update-slice_fusion.1
  8.3 0.9 constant_dynamic-update-slice_fusion
  9.2 0.7 copy-done.3
  9.9 0.0 all-gather.6.cloned.1.call-update
  9.9 0.7 fusion.45
  10.6 1.3 fusion.24
  11.9 0.1 copy.28
  12.0 0.1 reduce_window_sum.11
  12.0 0.1 copy.29
  12.1 0.7 select_reduce_fusion
  12.8 0.7 iota_compare_fusion.2
  13.5 1.4 convolution_convert_fusion.1
  14.8 0.5 copy.30
  15.4 18.6 %all_to_all.15 = bf16[16,4,5120]{2,1,0:T(4,128)(2,1)S(1)} all-to-all(bf16[16,4,5120]{2,1,0:T(4,128)(2,1)S(1)} %copy.30), channel_id=1, replica_groups=mesh['ctx'=16,'exp'=16] {'exp'}, dimensions={0} | all-to-all | bytes 1310720 | tf_op jit(solution)/shard_map/all_to_all | solution.py:96
  34.0 1.0 stack_reshape.2
  35.0 6.4 %stack.24 = bf16[16,64,5120]{2,1,0:T(8,128)(2,1)} broadcast(bf16[64,5120]{1,0:T(8,128)(2,1)} %stack_reshape.2), dimensions={1,2} | broadcast | bytes 11141120 | tf_op jit(solution)/shard_map/stack | solution.py:99
  41.4 8.7 %all-to-all-start.1 = ((bf16[16,64,5120]{2,1,0:T(8,128)(2,1)}), bf16[16,64,5120]{2,1,0:T(8,128)(2,1)}, u32[]{:S(2)}, u32[]{:S(2)}) async-start(bf16[16,64,5120]{2,1,0:T(8,128)(2,1)} %stack.24), calls=%async_computation.1 | async-start | bytes 20971520 | tf_op jit(solution)/shard_map/all_to_all | solution.py:98
  50.2 0.0 all-gather.4.cloned.1.call-start
  50.2 0.1 fusion.46
  50.3 0.6 gather_fusion
  51.0 29.0 %all-gather.6.cloned.1.call-done = bf16[32,64,1024]{2,1,0:T(8,128)(2,1)} async-done(((bf16[2,64,1024]{2,1,0:T(8,128)(2,1)}), bf16[32,64,1024]{2,1,0:T(8,128)(2,1)}) %all-gather.6.cloned.1.call-update) | async-done | bytes 4194320 | tf_op jit(solution)/shard_map/all_gather | solution.py:25
  80.0 2.8 gather_fusion.1
  82.8 0.8 pad_maximum_fusion.1
  83.6 0.0 all-gather.4.cloned.1.call-update
  83.6 0.0 reduce-scatter.2.cloned.1.call-start
  83.7 195.6 %all-to-all-done.1 = bf16[16,64,5120]{2,1,0:T(8,128)(2,1)} async-done(((bf16[16,64,5120]{2,1,0:T(8,128)(2,1)}), bf16[16,64,5120]{2,1,0:T(8,128)(2,1)}, u32[]{:S(2)}, u32[]{:S(2)}) %all-to-all-start.1) | async-done | bytes 10485792 | tf_op jit(solution)/shard_map/all_to_all | solution.py:98
  279.3 8.6 %fusion.11 = f32[1024,256]{1,0:T(8,128)} fusion(bf16[1024,5120]{1,0:T(8,128)(2,1)} %bitcast.17, bf16[1,5120,256]{2,1,0:T(8,128)(2,1)} %param.17), kind=kOutput, calls=%fused_computation.20 | convolution fusion | flops 2684354560 | bytes 14155776 | tf_op jit(solution)/shard_map/dot_general | solution.py:103
  287.8 21.0 %convolution_convert_fusion = bf16[1024,5120]{1,0:T(8,128)(2,1)} fusion(bf16[1,256,5120]{2,1,0:T(8,128)(2,1)S(1)} %copy-done, bf16[1024,5120]{1,0:T(8,128)(2,1)} %bitcast.17, bf16[1,5120,256]{2,1,0:T(8,128)(2,1)} %param.18, f32[1024,256]{1,0:T(8,128)} %fusion.11), kind=kOutput, calls=%fused_computation.9 | convolution fusion | flops 5375524864 | bytes 27262976 | tf_op jit(solution)/shard_map/dot_general | solution.py:107
  308.9 1.1 copy-done.5
  309.9 0.8 reshape.252
  310.7 0.1 add_compare_fusion
  310.8 0.1 iota_compare_fusion
  310.9 0.1 broadcast_in_dim.27
  311.1 0.0 all-gather.4.cloned.1.call-done
  311.1 3.9 fusion.57
  315.0 3.9 fusion.7
  319.0 6.3 %copy.25 = bf16[2,2048,512]{1,2,0:T(8,128)(2,1)} copy(bf16[2,2048,512]{2,1,0:T(8,128)(2,1)} %get-tuple-element.3) | data formatting | bytes 8388608 | tf_op jit(solution)/shard_map/slice | solution.py:41
  325.3 6.4 %copy.22 = bf16[2,2048,512]{1,2,0:T(8,128)(2,1)} copy(bf16[2,2048,512]{2,1,0:T(8,128)(2,1)} %get-tuple-element.2) | data formatting | bytes 8388608 | tf_op jit(solution)/shard_map/slice | solution.py:38
  331.6 13.4 %fusion = (f32[2,4,5,64]{3,2,1,0:T(8,128)S(1)}, f32[2,4,2048,64,5]{2,3,4,1,0:T(8,128)}) fusion(pred[2,64,2048]{2,1,0:T(8,128)(4,1)S(1)} %pad_add_fusion, bf16[2,2048,4,128,1]{1,3,4,2,0:T(8,128)(2,1)} %bitcast.71, bf16[2,64,4,5,128]{4,3,2,1,0:T(8,128)(2,1)S(1)} %reshape.252), kind=kOutput, calls=%fused_computation.4 | convolution fusion | flops 1357903360 | bytes 26093568 | tf_op jit(solution)/shard_map/prhgd,pkhd->phgrk/dot_general | solution.py:45
  345.1 11.6 %fusion.1 = f32[2,4,5,64]{3,2,1,0:T(8,128)} fusion(f32[2,4,2048,64,5]{2,3,4,1,0:T(8,128)} %get-tuple-element.7, f32[2,4,5,64]{3,2,1,0:T(8,128)S(1)} %broadcast_maximum_fusion, pred[2,64,2048]{2,1,0:T(8,128)(4,1)S(1)} %pad_add_fusion), kind=kLoop, calls=%fused_computation.5 | loop fusion | flops 26211840 | bytes 21254144 | tf_op jit(solution)/shard_map/reduce_sum | solution.py:59
  356.7 24.5 %reduce-scatter.2.cloned.1.call-done = bf16[64,5120]{1,0:T(8,128)(2,1)} async-done(((bf16[1024,5120]{1,0:T(8,128)(2,1)}), bf16[64,5120]{1,0:T(8,128)(2,1)}) %reduce-scatter.2.cloned.1.call-update) | async-done | bytes 655376 | tf_op jit(solution)/shard_map/reduce_scatter | solution.py:106
  381.2 2.3 reshape.255
  383.5 7.3 %all-to-all-start.2 = ((bf16[16,4,5120]{2,1,0:T(4,128)(2,1)}), bf16[16,4,5120]{2,1,0:T(4,128)(2,1)S(1)}, u32[]{:S(2)}, u32[]{:S(2)}) async-start(bf16[16,4,5120]{2,1,0:T(4,128)(2,1)} %reshape.255), calls=%async_computation.3 | async-start | bytes 1310720 | tf_op jit(solution)/shard_map/all_to_all | solution.py:114
  390.8 10.9 %divide_convert_fusion = bf16[2,64,4,5,128]{4,1,3,2,0:T(8,128)(2,1)S(1)} fusion(bf16[2,2048,4,128,1]{1,3,4,2,0:T(8,128)(2,1)} %bitcast.72, f32[2,4,2048,64,5]{2,3,4,1,0:T(8,128)} %get-tuple-element.7, f32[2,4,5,64]{3,2,1,0:T(8,128)} %copy-done.6, pred[2,64,2048]{2,1,0:T(8,128)(4,1)S(1)} %pad_add_fusion, f32[2,64,4,5]{1,3,2,0:T(8,128)} %bitcast.73), kind=kOutput, calls=%fused_computation.23 | convolution fusion | flops 1369047040 | bytes 26103808 | tf_op jit(solution)/shard_map/phgrk,pkhd->phgrd/dot_general | solution.py:60
  401.7 1.5 copy.27
  403.2 2.6 convert_element_type.51
  405.7 1.0 fusion.6
  (23 shorter events, 0.2 us)
Async XLA Ops:
  7.2 280.7 %copy-start = (bf16[1,256,5120]{2,1,0:T(8,128)(2,1)S(1)}, bf16[1,256,5120]{2,1,0:T(8,128)(2,1)}, u32[]{:S(2)}) copy-start(bf16[1,256,5120]{2,1,0:T(8,128)(2,1)} %param.19) | copy-start | bytes 7864324
  7.2 72.8 %all-gather.6.cloned.1.call-start = ((), (), s32[]{:S(2)}) async-start(), calls=%async_computation.6 | async-start | bytes 4456448 | tf_op jit(solution)/shard_map/all_gather | solution.py:25
  9.2 0.7 copy-start.3
  41.4 8.9 %copy-start.2 = (s32[32]{0:T(128)S(1)}, s32[32]{0:T(128)}, u32[]{:S(2)}) copy-start(s32[32]{0:T(128)} %param.13) | copy-start | bytes 388
  41.4 41.3 %copy-start.4 = (bf16[2,64,1024]{2,1,0:T(8,128)(2,1)S(1)}, bf16[2,64,1024]{2,1,0:T(8,128)(2,1)}, u32[]{:S(2)}) copy-start(bf16[2,64,1024]{2,1,0:T(8,128)(2,1)} %copy-done.3) | copy-start | bytes 786436
  41.4 237.9 %all-to-all-start.1 = ((bf16[16,64,5120]{2,1,0:T(8,128)(2,1)}), bf16[16,64,5120]{2,1,0:T(8,128)(2,1)}, u32[]{:S(2)}, u32[]{:S(2)}) async-start(bf16[16,64,5120]{2,1,0:T(8,128)(2,1)} %stack.24), calls=%async_computation.1 | async-start | bytes 20971520 | tf_op jit(solution)/shard_map/all_to_all | solution.py:98
  50.2 260.9 %all-gather.4.cloned.1.call-start = ((), (), s32[]{:S(2)}) async-start(), calls=%async_computation.4 | async-start | bytes 8912896 | tf_op jit(solution)/shard_map/all_gather | solution.py:32
  83.6 297.5 %reduce-scatter.2.cloned.1.call-start = ((), (), s32[]{:S(2)}) async-start(), calls=%async_computation.5 | async-start | bytes 11141120 | tf_op jit(solution)/shard_map/reduce_scatter | solution.py:106
  308.8 1.1 copy-start.5
  345.1 11.6 %copy-start.6 = (f32[2,4,5,64]{3,2,1,0:T(8,128)}, f32[2,4,5,64]{3,2,1,0:T(8,128)S(1)}, u32[]{:S(2)}) copy-start(f32[2,4,5,64]{3,2,1,0:T(8,128)S(1)} %broadcast_maximum_fusion) | copy-start | bytes 30724
  383.5 22.2 %all-to-all-start.2 = ((bf16[16,4,5120]{2,1,0:T(4,128)(2,1)}), bf16[16,4,5120]{2,1,0:T(4,128)(2,1)S(1)}, u32[]{:S(2)}, u32[]{:S(2)}) async-start(bf16[16,4,5120]{2,1,0:T(4,128)(2,1)} %reshape.255), calls=%async_computation.3 | async-start | bytes 1310720 | tf_op jit(solution)/shard_map/all_to_all | solution.py:114
  390.8 16.0 %copy-start.1 = (bf16[1,256,5120]{2,1,0:T(8,128)(2,1)S(1)}, bf16[1,256,5120]{2,1,0:T(8,128)(2,1)}, u32[]{:S(2)}) copy-start(bf16[1,256,5120]{2,1,0:T(8,128)(2,1)} %param.19) | copy-start | bytes 7864324
Sparse Core Ops, SparseCore 0:
  10.4 69.5 all-gather.5
  83.7 84.0 all-gather.3
  309.0 72.1 reduce-scatter.1
